TPU v7x, 256 devices: a whole 4x4x8 slice. The times are simulated.
256 devices in a mesh: dp: 16 (over x, y), tensor: 16 (over z, core).
Axes of the slice: x: 4, y: 4, z: 8, core: 2. Of those that a mesh axis runs over, the one named last changes fastest.
Arguments:
- tokens: bfloat16 [8192, 8192], P(('dp', 'tensor')), may hold values from -6 to 6
- w_query: bfloat16 [8192, 8192], P(None, 'tensor'), may hold values from -0.0625 to 0.0625
- cotangent: bfloat16 [8192, 8192], P('dp', 'tensor'), may hold values from -6 to 6
- task_embed: bfloat16 [128, 1024], replicated, may hold values from -6 to 6
- w_hidden: bfloat16 [1024, 512], P(None, 'tensor'), may hold values from -0.1875 to 0.1875
- head_a: bfloat16 [512, 16, 8192], P(None, 'dp', 'tensor'), may hold values from -0.0234375 to 0.0234375
- head_b: bfloat16 [512, 16, 8192], P(None, 'dp', 'tensor'), may hold values from -0.0234375 to 0.0234375
- block_task: int32 [16], replicated, may hold values from 0 to 127
Outputs:
- output: bfloat16 [8192, 8192], P('dp', 'tensor')
- grad_tokens: bfloat16 [8192, 8192], P(('dp', 'tensor'))
- grad_head_a: bfloat16 [512, 16, 8192], P(None, 'dp', 'tensor')
- grad_head_b: bfloat16 [512, 16, 8192], P(None, 'dp', 'tensor')
All inputs are finite; a program needn't handle non-finite values.
Results may differ from a plain program's by a relative error of at most 0.0077.
Values may be sent and summed in bfloat16 or wider, within the bound.
No kernel may reach another device: no remote copies, remote signals or barrier semaphores. Data moves between devices by JAX's collectives and lax.ppermute only.
A program may use at most 128 MiB of HBM per device.

v0:
```python
import jax
import jax.numpy as jnp
from jax import lax
from jax.sharding import PartitionSpec as P


def local(tokens, w_query, cotangent, task_embed, w_hidden, head_a, head_b, block_task):
    single_float = jnp.float32
    brain_half_float = jnp.bfloat16
    n_groups = lax.axis_size("dp")
    n_shards = lax.axis_size("tensor")
    shard = lax.axis_index("tensor")
    group = lax.axis_index("dp")
    hid_count, rank_rows, width = head_a.shape
    ntasks = task_embed.shape[0]
    blocks = block_task.shape[0]
    per_group = blocks // n_groups
    hid_part = jax.nn.silu(
        jnp.dot(task_embed, w_hidden, preferred_element_type=single_float)
    ).astype(brain_half_float)
    hidden = lax.all_gather(hid_part, "tensor", axis=1, tiled=True)
    flat_a = head_a.reshape(hid_count, rank_rows * width)
    flat_b = head_b.reshape(hid_count, rank_rows * width)
    mine = lax.dynamic_slice_in_dim(block_task, group * per_group, per_group)
    task_ids = jnp.arange(ntasks, dtype=jnp.int32)
    gen_a = (
        jnp.dot(hidden, flat_a, preferred_element_type=single_float)
        .astype(brain_half_float)
        .reshape(ntasks, rank_rows, width)
    )
    gen_b = (
        jnp.dot(hidden, flat_b, preferred_element_type=single_float)
        .astype(brain_half_float)
        .reshape(ntasks, rank_rows, width)
    )
    all_tasks_down, all_tasks_up = (
        lax.all_gather(gen_a, "dp", axis=1, tiled=True),
        lax.all_gather(gen_b, "dp", axis=1, tiled=True),
    )
    task_selector = (mine[:, None] == task_ids[None, :]).astype(brain_half_float)
    adapter_down_weight = jnp.einsum(
        "yg,ghi->yhi", task_selector, all_tasks_down, preferred_element_type=single_float
    ).astype(brain_half_float)
    adapter_up_weight = jnp.einsum(
        "yg,ghi->yhi", task_selector, all_tasks_up, preferred_element_type=single_float
    ).astype(brain_half_float)
    rank = adapter_down_weight.shape[1]
    whole = lax.all_gather(tokens, "tensor", axis=0, tiled=True)
    rows_all, model_width = whole.shape
    block = rows_all // per_group
    rows_dev = rows_all // n_shards
    block_inputs = whole.reshape(per_group, block, model_width)
    input_columns = lax.dynamic_slice_in_dim(block_inputs, shard * width, width, 2)
    frozen_output = jnp.dot(whole, w_query, preferred_element_type=single_float)
    down_portion = jnp.einsum(
        "grs,gps->grp", input_columns, adapter_down_weight, preferred_element_type=single_float
    )
    down_projection = lax.psum(down_portion, "tensor")
    down_low_rank = down_projection.astype(brain_half_float)
    low_rank_update = jnp.einsum(
        "elm,emn->eln", down_low_rank, adapter_up_weight, preferred_element_type=single_float
    ).reshape(rows_all, width)
    output = (frozen_output + low_rank_update).astype(brain_half_float)
    block_output_grads = cotangent.reshape(per_group, block, width)
    backward_portion = jnp.einsum(
        "grs,gps->grp", block_output_grads, adapter_up_weight, preferred_element_type=single_float
    )
    backward_input = lax.psum(backward_portion, "tensor")
    backward_low_rank = backward_input.astype(brain_half_float)
    grad_sum = lax.psum_scatter(
        lax.dot_general(
            cotangent, w_query, (((1,), (1,)), ((), ())), preferred_element_type=single_float
        ),
        "tensor",
        scatter_dimension=0,
        tiled=True,
    )
    full_a = lax.all_gather(adapter_down_weight, "tensor", axis=2, tiled=True)
    first = shard * rows_dev
    which = first // block
    a_here = lax.dynamic_index_in_dim(full_a, which, 0, keepdims=False)
    back_rows = lax.dynamic_slice_in_dim(
        backward_low_rank.reshape(rows_all, rank), first, rows_dev, 0
    )
    grad_sum = grad_sum + jnp.dot(back_rows, a_here, preferred_element_type=single_float)
    grad_tokens = grad_sum.astype(brain_half_float)
    scale_average = 1.0 / block
    down_gradient = (
        jnp.einsum(
            "evr,evx->erx", backward_low_rank, input_columns, preferred_element_type=single_float
        )
        * scale_average
    ).astype(brain_half_float)
    up_gradient = (
        jnp.einsum(
            "evr,evx->erx", down_low_rank, block_output_grads, preferred_element_type=single_float
        )
        * scale_average
    ).astype(brain_half_float)
    task_down_weight = jnp.einsum(
        "xh,xui->hui", task_selector, down_gradient, preferred_element_type=single_float
    )
    task_up_weight = jnp.einsum(
        "xh,xui->hui", task_selector, up_gradient, preferred_element_type=single_float
    )
    own_a, own_b = (
        lax.psum_scatter(
            task_down_weight.astype(jnp.bfloat16), "dp", scatter_dimension=1, tiled=True
        ).astype(jnp.float32),
        lax.psum_scatter(
            task_up_weight.astype(jnp.bfloat16), "dp", scatter_dimension=1, tiled=True
        ).astype(jnp.float32),
    )
    hid_f = hidden.astype(single_float)
    head_grad_a = lax.dot_general(
        hid_f,
        own_a.reshape(ntasks, rank_rows * width),
        (((0,), (0,)), ((), ())),
        precision=lax.Precision.HIGHEST,
    )
    head_grad_b = lax.dot_general(
        hid_f,
        own_b.reshape(ntasks, rank_rows * width),
        (((0,), (0,)), ((), ())),
        precision=lax.Precision.HIGHEST,
    )
    grad_head_a = head_grad_a.reshape(hid_count, rank_rows, width).astype(brain_half_float)
    grad_head_b = head_grad_b.reshape(hid_count, rank_rows, width).astype(brain_half_float)
    return (output, grad_tokens, grad_head_a, grad_head_b)


def solution(mesh):
    return jax.shard_map(
        local,
        mesh=mesh,
        in_specs=(
            P(("dp", "tensor"), None),
            P(None, "tensor"),
            P("dp", "tensor"),
            P(),
            P(None, "tensor"),
            P(None, "dp", "tensor"),
            P(None, "dp", "tensor"),
            P(),
        ),
        out_specs=(
            P("dp", "tensor"),
            P(("dp", "tensor"), None),
            P(None, "dp", "tensor"),
            P(None, "dp", "tensor"),
        ),
        check_vma=False,
    )
```

profile of v0, /device:TPU:2, one launch (start us, length us, event | category | flops | bytes accessed | tf_op | source)
XLA Modules:
  0.0 520.4 jit_solution(2591239751184445774)
XLA Ops:
  7.2 0.0 copy-start
  7.2 0.0 all-gather.9.cloned.1.call-start
  7.2 1.2 multiply_convert_fusion.2
  8.4 20.3 %all_gather.16 = bf16[128,512]{0,1:T(8,128)(2,1)S(1)} all-gather(bf16[128,32]{0,1:T(8,128)(2,1)S(1)} %multiply_convert_fusion.2), channel_id=1, replica_groups=mesh['dp'=16,'tensor'=16] {'tensor'}, dimensions={1}, use_global_device_ids=true | all-gather | bytes 139264 | tf_op jit(solution)/shard_map/all_gather | solution.py:21
  28.8 2.0 convolution_convert_fusion.3
  30.7 0.0 all-gather.9.cloned.1.call-update
  30.7 0.0 all-gather.11.cloned.1.call-start
  30.8 2.0 convolution_convert_fusion.2
  32.7 0.0 all-gather.11.cloned.1.call-update
  32.8 0.0 all-gather.7.cloned.1.call-start
  32.8 0.7 all-gather.7.cloned.1.call-update
  33.5 0.0 reduce-scatter.10.cloned.1.call-start
  33.6 1.2 dynamic_slice.11
  34.8 0.6 fusion.29
  35.5 45.3 %all-gather.9.cloned.1.call-done = bf16[128,8192]{1,0:T(8,128)(2,1)} async-done(((bf16[128,512]{1,0:T(8,128)(2,1)}), bf16[128,8192]{1,0:T(8,128)(2,1)}) %all-gather.9.cloned.1.call-update) | async-done | bytes 2097168 | tf_op jit(solution)/shard_map/all_gather | solution.py:37
  80.7 2.6 fusion.4
  83.3 51.8 %all-gather.11.cloned.1.call-done = bf16[128,8192]{1,0:T(8,128)(2,1)} async-done(((bf16[128,512]{1,0:T(8,128)(2,1)}), bf16[128,8192]{1,0:T(8,128)(2,1)}) %all-gather.11.cloned.1.call-update) | async-done | bytes 2097168 | tf_op jit(solution)/shard_map/all_gather | solution.py:38
  135.2 2.6 fusion.1
  137.8 0.0 copy-done
  137.8 0.2 convolution_bitcast_fusion
  138.0 54.6 %all-gather.7.cloned.1.call-done = bf16[512,8192]{1,0:T(8,128)(2,1)} async-done(((bf16[32,8192]{1,0:T(8,128)(2,1)}), bf16[512,8192]{1,0:T(8,128)(2,1)}) %all-gather.7.cloned.1.call-update) | async-done | bytes 8388624 | tf_op jit(solution)/shard_map/all_gather | solution.py:48
  192.6 1.3 convolution_bitcast_fusion.1
  193.9 46.9 %all-reduce.2 = (bf16[1,512,16]{1,2,0:T(8,128)(2,1)S(1)}, bf16[1,512,16]{1,2,0:T(8,128)(2,1)S(1)}) all-reduce(f32[1,512,16]{1,2,0:T(8,128)S(1)} %convolution_bitcast_fusion.1, f32[1,512,16]{1,2,0:T(8,128)S(1)} %convolution_bitcast_fusion), channel_id=1, replica_groups=mesh['dp'=16,'tensor'=16] {'tensor'}, use_global_device_ids=true, to_apply=%region_0.1 | all-reduce | flops 16384 | bytes 98304 | tf_op jit(solution)/shard_map/psum | solution.py:58
  240.8 0.2 fusion.13
  240.9 1.2 fusion.11
  242.2 3.5 multiply_convert_fusion
  245.6 0.0 reduce-scatter.10.cloned.1.call-update
  245.7 0.0 reduce-scatter.12.cloned.1.call-start
  245.7 0.5 reduce-scatter.12.cloned.1.call-update
  246.3 0.0 reduce-scatter.8.cloned.1.call-start
  246.3 11.6 %fusion.36 = f32[512,8192]{1,0:T(8,128)} fusion(bf16[512,512]{1,0:T(8,128)(2,1)S(1)} %copy-done, bf16[8192,512]{1,0:T(8,128)(2,1)} %param.9), kind=kOutput, calls=%fused_computation.52 | convolution fusion | flops 4294967296 | bytes 25690112 | tf_op jit(solution)/shard_map/dot_general | solution.py:71
  257.9 0.0 reduce-scatter.8.cloned.1.call-update
  257.9 14.9 %all-gather.2 = bf16[16,8192]{1,0:T(8,128)(2,1)S(1)} all-gather(bf16[16,512]{1,0:T(8,128)(2,1)S(1)} %bitcast.73), channel_id=4, replica_groups=mesh['dp'=16,'tensor'=16] {'tensor'}, dimensions={1}, use_global_device_ids=true | all-gather | bytes 278528 | tf_op jit(solution)/shard_map/all_gather | solution.py:78
  272.8 9.5 %fusion.35 = f32[512,512]{1,0:T(8,128)S(1)} fusion(bf16[512,8192]{1,0:T(8,128)(2,1)} %all-gather.7.cloned.1.call-done, bf16[8192,512]{1,0:T(8,128)(2,1)} %param.9), kind=kOutput, calls=%fused_computation.51 | convolution fusion | flops 4294967296 | bytes 17825792 | tf_op jit(solution)/shard_map/dot_general | solution.py:54
  282.3 1.1 fusion.7
  283.4 42.0 %reduce-scatter.10.cloned.1.call-done = bf16[128,1,512]{2,0,1:T(8,128)(2,1)} async-done(((bf16[128,16,512]{2,0,1:T(8,128)(2,1)}), bf16[128,1,512]{2,0,1:T(8,128)(2,1)}) %reduce-scatter.10.cloned.1.call-update) | async-done | bytes 131088
  325.4 2.0 fusion.8
  327.4 81.0 %reduce-scatter.12.cloned.1.call-done = bf16[128,1,512]{2,0,1:T(8,128)(2,1)} async-done(((bf16[128,16,512]{2,0,1:T(8,128)(2,1)}), bf16[128,1,512]{2,0,1:T(8,128)(2,1)}) %reduce-scatter.12.cloned.1.call-update) | async-done | bytes 131088
  408.5 2.0 fusion.9
  410.4 100.7 %reduce-scatter.8.cloned.1.call-done = f32[32,8192]{1,0:T(8,128)} async-done(((f32[512,8192]{1,0:T(8,128)}), f32[32,8192]{1,0:T(8,128)}) %reduce-scatter.8.cloned.1.call-update) | async-done | bytes 1048592 | tf_op jit(solution)/shard_map/reduce_scatter | solution.py:70
  511.1 2.4 fusion
  (1 shorter events, 0.0 us)
Async XLA Ops:
  7.2 130.6 %copy-start = (bf16[512,512]{1,0:T(8,128)(2,1)S(1)}, bf16[512,512]{1,0:T(8,128)(2,1)}, u32[]{:S(2)}) copy-start(bf16[512,512]{1,0:T(8,128)(2,1)} %param.10) | copy-start | bytes 1572868
  7.2 73.5 %all-gather.9.cloned.1.call-start = ((), (), s32[]{:S(2)}) async-start(), calls=%async_computation.5 | async-start | bytes 2228224 | tf_op jit(solution)/shard_map/all_gather | solution.py:37
  30.7 104.4 %all-gather.11.cloned.1.call-start = ((), (), s32[]{:S(2)}) async-start(), calls=%async_computation.6 | async-start | bytes 2228224 | tf_op jit(solution)/shard_map/all_gather | solution.py:38
  32.8 159.8 %all-gather.7.cloned.1.call-start = ((), (), s32[]{:S(2)}) async-start(), calls=%async_computation.3 | async-start | bytes 8912896 | tf_op jit(solution)/shard_map/all_gather | solution.py:48
  33.5 291.9 %reduce-scatter.10.cloned.1.call-start = ((), (), s32[]{:S(2)}) async-start(), calls=%async_computation.7 | async-start | bytes 2228224
  245.7 162.8 %reduce-scatter.12.cloned.1.call-start = ((), (), s32[]{:S(2)}) async-start(), calls=%async_computation.8 | async-start | bytes 2228224
  246.3 264.9 %reduce-scatter.8.cloned.1.call-start = ((), (), s32[]{:S(2)}) async-start(), calls=%async_computation.4 | async-start | bytes 17825792 | tf_op jit(solution)/shard_map/reduce_scatter | solution.py:70
Sparse Core Ops, SparseCore 0:
  30.9 49.8 all-gather.8
  83.7 51.4 all-gather.10
  137.0 55.5 all-gather.6
  245.8 79.6 reduce-scatter.9
  328.8 79.5 reduce-scatter.11
  410.9 100.2 reduce-scatter.7
where the time goes:
time: 521 us; the launch traced here: 520 us
  waiting for transfers between devices  377 us (72%)
  blocking collectives  82.1 us (16%)
  matrix products  41.8 us (8%)
  between operations  14.2 us (3%)
    unnamed x8, waiting for transfers between devices  124 us
    reduce_scatter x1, waiting for transfers between devices, local(): lax.psum_scatter(lax.dot_general(cotangent, w_query, (((1,), (1,)), ((),...  101 us
    all_gather x1, waiting for transfers between devices, local(): whole = lax.all_gather(tokens, 'tensor', axis=0, tiled=True)  54.6 us
    all_gather x1, waiting for transfers between devices, local(): lax.all_gather(gen_b, 'dp', axis=1, tiled=True)  51.8 us
    psum x1, blocking collectives, local(): down_projection = lax.psum(down_portion, 'tensor')  46.9 us
    all_gather x1, waiting for transfers between devices, local(): lax.all_gather(gen_a, 'dp', axis=1, tiled=True)  45.3 us
    all_gather x1, blocking collectives, local(): hidden = lax.all_gather(hid_part, 'tensor', axis=1, tiled=True)  20.3 us
    all_gather x1, blocking collectives, local(): full_a = lax.all_gather(adapter_down_weight, 'tensor', axis=2, tiled=True)  14.9 us
  transfers between devices with their start and end apart: 6, of which 6 were waited for; matrix products, arithmetic and copies ran while one was open for 7% of the time, Pallas kernels for 0%

commit v1 on v0

--- a/solution.py
+++ b/solution.py
@@ -55,7 +55,7 @@
     down_portion = jnp.einsum(
         "grs,gps->grp", input_columns, adapter_down_weight, preferred_element_type=single_float
     )
-    down_projection = lax.psum(down_portion, "tensor")
+    down_projection = jnp.sum(lax.all_gather(down_portion, "tensor"), axis=0)
     down_low_rank = down_projection.astype(brain_half_float)
     low_rank_update = jnp.einsum(
         "elm,emn->eln", down_low_rank, adapter_up_weight, preferred_element_type=single_float

time: 521 us -> 492 us (0.944)
  waiting for transfers between devices: 377 us -> 326 us
  blocking collectives: 82.1 us -> 104 us
    all_gather x1, waiting for transfers between devices: 54.6 us -> 4.11 us  [local(): whole = lax.all_gather(tokens, 'tensor', axis=0, tiled=True)]
    all_gather x0 -> x1, blocking collectives: none -> 16.9 us  [local(): down_projection = jnp.sum(lax.all_gather(down_portion, 'tensor'), axis=0)]
where the time goes in v1:
time: 492 us; the launch traced here: 491 us
  waiting for transfers between devices  326 us (66%)
  blocking collectives  104 us (21%)
  matrix products  41.8 us (8%)
  between operations  14.2 us (3%)
    unnamed x8, waiting for transfers between devices  124 us
    reduce_scatter x1, waiting for transfers between devices, local(): lax.psum_scatter(lax.dot_general(cotangent, w_query, (((1,), (1,)), ((),...  101 us
    all_gather x1, waiting for transfers between devices, local(): lax.all_gather(gen_b, 'dp', axis=1, tiled=True)  51.8 us
    psum x1, blocking collectives, local(): backward_input = lax.psum(backward_portion, 'tensor')  51 us
    all_gather x1, waiting for transfers between devices, local(): lax.all_gather(gen_a, 'dp', axis=1, tiled=True)  45.3 us
    all_gather x1, blocking collectives, local(): hidden = lax.all_gather(hid_part, 'tensor', axis=1, tiled=True)  20.3 us
    all_gather x1, blocking collectives, local(): down_projection = jnp.sum(lax.all_gather(down_portion, 'tensor'), axis=0)  16.9 us
    all_gather x1, blocking collectives, local(): full_a = lax.all_gather(adapter_down_weight, 'tensor', axis=2, tiled=True)  15.4 us
  transfers between devices with their start and end apart: 6, of which 6 were waited for; matrix products, arithmetic and copies ran while one was open for 7% of the time, Pallas kernels for 0%

profile of v1, /device:TPU:2, one launch (start us, length us, event | category | flops | bytes accessed | tf_op | source)
XLA Modules:
  0.0 491.3 jit_solution(15709266019836484573)
XLA Ops:
  7.2 0.0 copy-start
  7.2 0.0 all-gather.10.cloned.1.call-start
  7.2 1.2 multiply_convert_fusion.2
  8.4 20.3 %all_gather.22 = bf16[128,512]{0,1:T(8,128)(2,1)S(1)} all-gather(bf16[128,32]{0,1:T(8,128)(2,1)S(1)} %multiply_convert_fusion.2), channel_id=1, replica_groups=mesh['dp'=16,'tensor'=16] {'tensor'}, dimensions={1}, use_global_device_ids=true | all-gather | bytes 139264 | tf_op jit(solution)/shard_map/all_gather | solution.py:21
  28.8 2.0 convolution_convert_fusion.3
  30.7 0.0 all-gather.10.cloned.1.call-update
  30.7 0.0 all-gather.12.cloned.1.call-start
  30.8 2.0 convolution_convert_fusion.2
  32.7 0.0 all-gather.12.cloned.1.call-update
  32.8 0.0 all-gather.8.cloned.1.call-start
  32.8 0.7 all-gather.8.cloned.1.call-update
  33.5 0.0 reduce-scatter.10.cloned.1.call-start
  33.6 1.2 dynamic_slice.11
  34.8 0.6 fusion.28
  35.5 45.3 %all-gather.10.cloned.1.call-done = bf16[128,8192]{1,0:T(8,128)(2,1)} async-done(((bf16[128,512]{1,0:T(8,128)(2,1)}), bf16[128,8192]{1,0:T(8,128)(2,1)}) %all-gather.10.cloned.1.call-update) | async-done | bytes 2097168 | tf_op jit(solution)/shard_map/all_gather | solution.py:37
  80.7 2.6 fusion.4
  83.3 51.8 %all-gather.12.cloned.1.call-done = bf16[128,8192]{1,0:T(8,128)(2,1)} async-done(((bf16[128,512]{1,0:T(8,128)(2,1)}), bf16[128,8192]{1,0:T(8,128)(2,1)}) %all-gather.12.cloned.1.call-update) | async-done | bytes 2097168 | tf_op jit(solution)/shard_map/all_gather | solution.py:38
  135.2 2.6 fusion.1
  137.8 0.0 copy-done
  137.8 0.2 convolution_bitcast_fusion
  138.0 51.0 %psum.7 = bf16[1,512,16]{1,2,0:T(8,128)(2,1)S(1)} all-reduce(f32[1,512,16]{1,2,0:T(8,128)S(1)} %convolution_bitcast_fusion), channel_id=1, replica_groups=mesh['dp'=16,'tensor'=16] {'tensor'}, use_global_device_ids=true, to_apply=%region_2.3 | all-reduce | flops 8192 | bytes 49152 | tf_op jit(solution)/shard_map/psum | solution.py:68
  189.1 4.1 all-gather.8.cloned.1.call-done
  193.2 1.3 fusion.17
  194.4 16.9 %all-gather.1 = f32[8192,16]{0,1:T(8,128)S(1)} all-gather(f32[512,16]{0,1:T(8,128)S(1)} %fusion.17), channel_id=3, replica_groups=mesh['dp'=16,'tensor'=16] {'tensor'}, dimensions={0}, use_global_device_ids=true | all-gather | bytes 557056 | tf_op jit(solution)/shard_map/all_gather | solution.py:58
  211.3 0.3 copy.18
  211.6 0.1 bitcast_reduce_fusion
  211.7 0.2 fusion.13
  211.9 1.2 fusion.11
  213.1 3.5 multiply_convert_fusion
  216.6 0.0 reduce-scatter.10.cloned.1.call-update
  216.6 0.0 reduce-scatter.12.cloned.1.call-start
  216.6 0.5 reduce-scatter.12.cloned.1.call-update
  217.2 0.0 reduce-scatter.8.cloned.1.call-start
  217.2 11.6 %fusion.35 = f32[512,8192]{1,0:T(8,128)} fusion(bf16[512,512]{1,0:T(8,128)(2,1)S(1)} %copy-done, bf16[8192,512]{1,0:T(8,128)(2,1)} %param.9), kind=kOutput, calls=%fused_computation.51 | convolution fusion | flops 4294967296 | bytes 25690112 | tf_op jit(solution)/shard_map/dot_general | solution.py:71
  228.8 0.0 reduce-scatter.8.cloned.1.call-update
  228.9 15.4 %all-gather.3 = bf16[16,8192]{1,0:T(8,128)(2,1)S(1)} all-gather(bf16[16,512]{1,0:T(8,128)(2,1)S(1)} %bitcast.74), channel_id=5, replica_groups=mesh['dp'=16,'tensor'=16] {'tensor'}, dimensions={1}, use_global_device_ids=true | all-gather | bytes 278528 | tf_op jit(solution)/shard_map/all_gather | solution.py:78
  244.3 9.5 %fusion.34 = f32[512,512]{1,0:T(8,128)S(1)} fusion(bf16[512,8192]{1,0:T(8,128)(2,1)} %all-gather.8.cloned.1.call-done, bf16[8192,512]{1,0:T(8,128)(2,1)} %param.9), kind=kOutput, calls=%fused_computation.50 | convolution fusion | flops 4294967296 | bytes 17825792 | tf_op jit(solution)/shard_map/dot_general | solution.py:54
  253.8 1.1 fusion.7
  254.9 41.4 %reduce-scatter.10.cloned.1.call-done = bf16[128,1,512]{2,0,1:T(8,128)(2,1)} async-done(((bf16[128,16,512]{2,0,1:T(8,128)(2,1)}), bf16[128,1,512]{2,0,1:T(8,128)(2,1)}) %reduce-scatter.10.cloned.1.call-update) | async-done | bytes 131088
  296.3 2.0 fusion.8
  298.3 81.1 %reduce-scatter.12.cloned.1.call-done = bf16[128,1,512]{2,0,1:T(8,128)(2,1)} async-done(((bf16[128,16,512]{2,0,1:T(8,128)(2,1)}), bf16[128,1,512]{2,0,1:T(8,128)(2,1)}) %reduce-scatter.12.cloned.1.call-update) | async-done | bytes 131088
  379.4 2.0 fusion.9
  381.3 100.7 %reduce-scatter.8.cloned.1.call-done = f32[32,8192]{1,0:T(8,128)} async-done(((f32[512,8192]{1,0:T(8,128)}), f32[32,8192]{1,0:T(8,128)}) %reduce-scatter.8.cloned.1.call-update) | async-done | bytes 1048592 | tf_op jit(solution)/shard_map/reduce_scatter | solution.py:70
  482.1 2.4 fusion
  (1 shorter events, 0.0 us)
Async XLA Ops:
  7.2 130.6 %copy-start = (bf16[512,512]{1,0:T(8,128)(2,1)S(1)}, bf16[512,512]{1,0:T(8,128)(2,1)}, u32[]{:S(2)}) copy-start(bf16[512,512]{1,0:T(8,128)(2,1)} %param.10) | copy-start | bytes 1572868
  7.2 73.5 %all-gather.10.cloned.1.call-start = ((), (), s32[]{:S(2)}) async-start(), calls=%async_computation.5 | async-start | bytes 2228224 | tf_op jit(solution)/shard_map/all_gather | solution.py:37
  30.7 104.4 %all-gather.12.cloned.1.call-start = ((), (), s32[]{:S(2)}) async-start(), calls=%async_computation.6 | async-start | bytes 2228224 | tf_op jit(solution)/shard_map/all_gather | solution.py:38
  32.8 160.4 %all-gather.8.cloned.1.call-start = ((), (), s32[]{:S(2)}) async-start(), calls=%async_computation.3 | async-start | bytes 8912896 | tf_op jit(solution)/shard_map/all_gather | solution.py:48
  33.5 262.8 %reduce-scatter.10.cloned.1.call-start = ((), (), s32[]{:S(2)}) async-start(), calls=%async_computation.7 | async-start | bytes 2228224
  216.6 162.8 %reduce-scatter.12.cloned.1.call-start = ((), (), s32[]{:S(2)}) async-start(), calls=%async_computation.8 | async-start | bytes 2228224
  217.2 264.9 %reduce-scatter.8.cloned.1.call-start = ((), (), s32[]{:S(2)}) async-start(), calls=%async_computation.4 | async-start | bytes 17825792 | tf_op jit(solution)/shard_map/reduce_scatter | solution.py:70
Sparse Core Ops, SparseCore 0:
  30.9 49.8 all-gather.9
  83.7 51.4 all-gather.11
  137.0 56.1 all-gather.7
  216.7 79.5 reduce-scatter.9
  299.7 79.6 reduce-scatter.11
  381.8 100.2 reduce-scatter.7
